TPU v7x, 512 devices: a whole 4x8x8 slice. The times are simulated.
512 devices in a mesh: aux: 128 (over y, z, core), occ: 4 (over x).
Axes of the slice: x: 4, y: 8, z: 8, core: 2. Of those that a mesh axis runs over, the one named last changes fastest.
Arguments:
- factors: bfloat16 [256, 2048, 384], P('occ', 'aux'), may hold values from -0.5 to 0.5
- response: bfloat16 [256, 2048, 384], P('occ', 'aux'), may hold values from -0.5 to 0.5
- pattern: int32 [3, 3], replicated, may hold values 0 or 1
Outputs:
- exchange_k: float32 [384, 384], P('aux', 'occ')
All inputs are finite; a program needn't handle non-finite values.
Results may differ from a plain program's by a relative error of at most 0.0003.
Values sent between devices are 32-bit elements; how exact they have to be, the bound alone decides.
A program may use at most 64 MiB of HBM per device.

v0:
```python
import jax
import jax.numpy as jnp
from jax import lax
from jax.sharding import PartitionSpec as P


def shards(factors, response, pattern):
    nocc_dev, aux_dev, nbasis = factors.shape
    ground_rows = factors.reshape(nocc_dev * aux_dev, nbasis)
    response_rows = response.reshape(nocc_dev * aux_dev, nbasis)
    nblocks = pattern.shape[0]
    blk_width = nbasis // nblocks
    tile_table = pattern.astype(jnp.float32)
    own_cols = nbasis // lax.axis_size("occ")
    occ_index = lax.axis_index("occ")
    row_share = nbasis // lax.axis_size("aux")
    cross = lax.dot_general(
        ground_rows, response_rows, (((0,), (0,)), ((), ())), preferred_element_type=jnp.float32
    )
    block_ids = jnp.arange(row_share * lax.axis_size("aux"), dtype=jnp.int32) // blk_width
    onehot = (block_ids[:, None] == jnp.arange(nblocks, dtype=jnp.int32)[None, :]).astype(
        jnp.float32
    )
    picked = jnp.dot(onehot, tile_table, precision=lax.Precision.HIGHEST)
    own_rows = lax.psum_scatter(
        jnp.repeat(picked, blk_width, axis=1) * cross, "aux", scatter_dimension=0, tiled=True
    )
    turned = lax.all_to_all(own_rows, "aux", split_axis=1, concat_axis=0, tiled=True)
    own_rows = 0.5 * (own_rows + turned.T)
    summed = lax.psum(own_rows, "occ")
    result = lax.dynamic_slice_in_dim(summed, occ_index * own_cols, own_cols, 1)
    return result


def solution(mesh):
    in_specs = (P("occ", "aux", None), P("occ", "aux", None), P())
    out_specs = P("aux", "occ")
    return jax.shard_map(shards, mesh=mesh, in_specs=in_specs, out_specs=out_specs, check_vma=False)
```

profile of v0, /device:TPU:1, one launch (start us, length us, event | category | flops | bytes accessed | tf_op | source)
XLA Modules:
  0.0 252.7 jit_solution(10268984997288870804)
XLA Ops:
  6.5 0.0 copy-start
  6.5 0.0 copy-start.2
  6.5 0.0 all-reduce.3.cloned.1.call-start
  6.5 0.7 copy-done.2
  7.3 0.3 fusion.1
  7.6 0.0 copy-start.1
  7.6 0.1 broadcast_in_dim.2
  7.7 0.2 copy.12
  7.9 0.0 copy-done
  7.9 0.9 copy-done.1
  8.8 1.4 fusion
  10.2 0.0 all-reduce.3.cloned.1.call-update
  10.2 1.3 dynamic-slice
  12.1 198.7 %all-reduce.3.cloned.1.call-done = f32[384,384]{1,0:T(8,128)} async-done(((f32[384,384]{1,0:T(8,128)}), f32[384,384]{1,0:T(8,128)}) %all-reduce.3.cloned.1.call-update) | async-done | bytes 589840
  210.9 0.7 constant_dynamic-slice_fusion
  211.6 0.2 all_to_all.14
  211.8 0.8 copy.13
  212.7 8.8 %all-to-all-start = ((f32[3,128,3]{2,0,1:T(4,128)}), f32[3,128,3]{2,0,1:T(4,128)S(1)}, u32[]{:S(2)}, u32[]{:S(2)}) async-start(f32[3,128,3]{2,0,1:T(4,128)} %copy.13), calls=%async_computation | async-start | bytes 524288 | tf_op jit(solution)/shard_map/all_to_all | solution.py:28
  221.5 14.2 %all-to-all-done = f32[3,128,3]{2,0,1:T(4,128)S(1)} async-done(((f32[3,128,3]{2,0,1:T(4,128)}), f32[3,128,3]{2,0,1:T(4,128)S(1)}, u32[]{:S(2)}, u32[]{:S(2)}) %all-to-all-start) | async-done | bytes 4640 | tf_op jit(solution)/shard_map/all_to_all | solution.py:28
  235.7 0.1 reshape.23
  235.8 0.1 copy.15
  235.9 0.8 fusion.3
  236.7 8.5 %psum.7 = f32[3,384]{1,0:T(4,128)S(1)} all-reduce(f32[3,384]{1,0:T(4,128)S(1)} %fusion.3), channel_id=1, replica_groups=mesh['aux'=128,'occ'=4] {'occ'}, use_global_device_ids=true, to_apply=%region_1.2 | all-reduce | flops 1152 | bytes 9216 | tf_op jit(solution)/shard_map/psum | solution.py:30
  245.2 0.7 constant_dynamic-slice_fusion.1
  (1 shorter events, 0.0 us)
Async XLA Ops:
  6.5 1.4 copy-start
  6.5 0.8 copy-start.2
  6.5 204.3 %all-reduce.3.cloned.1.call-start = ((), (), s32[]{:S(2)}) async-start(), calls=%async_computation.1 | async-start | bytes 1179648
  7.6 1.2 copy-start.1
  212.7 23.1 %all-to-all-start = ((f32[3,128,3]{2,0,1:T(4,128)}), f32[3,128,3]{2,0,1:T(4,128)S(1)}, u32[]{:S(2)}, u32[]{:S(2)}) async-start(f32[3,128,3]{2,0,1:T(4,128)} %copy.13), calls=%async_computation | async-start | bytes 524288 | tf_op jit(solution)/shard_map/all_to_all | solution.py:28
Sparse Core Ops, SparseCore 0:
  10.6 200.1 all-reduce.2
where the time goes:
time: 255 us; the launch traced here: 253 us
  waiting for transfers between devices  213 us (84%)
  between operations  14.1 us (6%)
  starting transfers between devices  8.84 us (3%)
  blocking collectives  8.49 us (3%)
  local copies, waits for them, and re-layouts  5.79 us (2%)
    unnamed x2, waiting for transfers between devices  199 us
    all_to_all x1, waiting for transfers between devices, shards(): lax.all_to_all(own_rows, 'aux', split_axis=1, concat_axis=0, tiled=True)  14.2 us
    all_to_all x1, starting transfers between devices, shards(): lax.all_to_all(own_rows, 'aux', split_axis=1, concat_axis=0, tiled=True)  8.83 us
    psum x1, blocking collectives, shards(): summed = lax.psum(own_rows, 'occ')  8.49 us
  transfers between devices with their start and end apart: 2, of which 2 were waited for; matrix products, arithmetic and copies ran while one was open for 1% of the time, Pallas kernels for 0%

commit v1 on v0

v1 whole, which is shorter than its diff:
```python
import jax
import jax.numpy as jnp
from jax import lax
from jax.experimental import pallas as pl
from jax.experimental.pallas import tpu as pltpu
from jax.sharding import PartitionSpec as P

X, Y, Z, C = 4, 8, 8, 2
SUB = 3
N = 384
COLS = N // X
F32 = jnp.float32
FAR8 = (4, 3, 5, 2, 6, 1, 7)
FAR4 = (2, 1, 3)


def kernel(
    a_hbm, b_hbm, p_hbm, o_ref,
    a_v, b_v, p_s, t_v,
    pair_src, pair_dst,
    x0_src, x0_dst, y0_src, y0_dst, z0_src, z0_dst,
    y1_src, y1_dst, z1_src, z1_dst, x1_src, x1_dst,
    z2_src, z2_dst, x2_src, x2_dst, y2_src, y2_dst,
    load_sem, pair_send, pair_recv, send4, recv4, send8, recv8,
):
    aux = lax.axis_index("aux")
    x = lax.axis_index("occ")
    c = lax.rem(aux, C)
    z = lax.rem(lax.div(aux, C), Z)
    y = lax.div(aux, C * Z)

    def at(x_, y_, z_, c_):
        return ((y_ * Z + z_) * C + c_, x_)

    def on_x(k):
        return at(lax.rem(x + k, X), y, z, c)

    def on_y(k):
        return at(x, lax.rem(y + k, Y), z, c)

    def on_z(k):
        return at(x, y, lax.rem(z + k, Z), c)

    partner = at(x, y, z, 1 - c)

    rows = a_v.shape[0]
    half = rows // 2
    loads = []
    for h in range(2):
        part = pl.ds(h * half, half)
        for n, (src, dst) in enumerate(((a_hbm, a_v), (b_hbm, b_v))):
            loads.append(pltpu.make_async_copy(src.at[part], dst.at[part], load_sem.at[2 * h + n]))
    p_load = pltpu.make_async_copy(p_hbm, p_s, load_sem.at[4])
    for ld in loads:
        ld.start()
    p_load.start()

    barrier = pltpu.get_barrier_semaphore()
    greeted = [partner]
    greeted += [on_y(k) for k in FAR8] + [on_z(k) for k in FAR8] + [on_x(k) for k in FAR4]
    for who in greeted:
        pl.semaphore_signal(barrier, inc=1, device_id=who, device_id_type=pl.DeviceIdType.MESH)

    def dot_t(l, r):
        return lax.dot_general(l, r, (((0,), (0,)), ((), ())), preferred_element_type=F32)

    loads[0].wait()
    loads[1].wait()
    s = dot_t(a_v[:half], b_v[:half])
    loads[2].wait()
    loads[3].wait()
    s = s + dot_t(a_v[half:], b_v[half:])
    p_load.wait()
    nb = p_s.shape[0]
    blk = N // nb
    for i in range(nb):
        for j in range(nb):
            f_ij = 0.5 * p_s[i, j].astype(F32)
            f_ji = 0.5 * p_s[j, i].astype(F32)
            r_i, r_j = slice(i * blk, (i + 1) * blk), slice(j * blk, (j + 1) * blk)
            t_v[j, r_i, :] = f_ij * s[r_i, r_j] + f_ji * s[r_j, r_i].T

    def pack(i):
        for cc in range(C):
            for j in range(nb):
                lanes = slice(j * blk, (j + 1) * blk)
                if i == 2:
                    for zz in range(Z):
                        got = t_v[j, pl.ds(6 * zz + 3 * cc + i, 8, stride=48), :]
                        pair_src[i, cc, 8 * zz:8 * zz + 8, lanes] = got
                else:
                    pair_src[i, cc, :, lanes] = t_v[j, pl.ds(3 * cc + i, 64, stride=6), :]

    def remote(src, dst, ss, rs, who):
        return pltpu.make_async_remote_copy(
            src_ref=src, dst_ref=dst, send_sem=ss, recv_sem=rs,
            device_id=who, device_id_type=pl.DeviceIdType.MESH,
        )

    pair = {}
    pl.semaphore_wait(barrier, len(greeted))
    for i in (2, 1, 0):
        pack(i)
        pair[i] = remote(
            pair_src.at[i, 1 - c], pair_dst.at[i], pair_send.at[i], pair_recv.at[i], partner
        )
        pair[i].start()

    sent = []

    def ring8(slot, to, me, src, dst):
        out = {}
        for k in FAR8:
            cp = remote(
                src.at[lax.rem(me + k, 8)], dst.at[k - 1],
                send8.at[slot, k - 1], recv8.at[slot, k - 1], to(k),
            )
            cp.start()
            out[k] = cp
        sent.extend(out.values())
        return out

    def ring4(slot, src, dst):
        out = {}
        for k in FAR4:
            cp = remote(
                src(lax.rem(x + k, X)), dst.at[k - 1],
                send4.at[slot, k - 1], recv4.at[slot, k - 1], on_x(k),
            )
            cp.start()
            out[k] = cp
        sent.extend(out.values())
        return out

    def total(own, copies, dst):
        acc = own
        for k in sorted(copies, key=lambda n: min(n, len(copies) + 1 - n)):
            copies[k].wait_recv()
            acc = acc + dst[k - 1]
        return acc

    def quarter(v, xx):
        return pltpu.roll(v, (N - COLS * xx) % N, 1)[:, :128] if xx else v[:, :128]

    pair[2].wait_recv()
    z2_src[...] = (pair_src[2, c] + pair_dst[2]).reshape(8, 8, N)
    z2 = ring8(0, on_z, z, z2_src, z2_dst)
    pair[1].wait_recv()
    y1_src[...] = (pair_src[1, c] + pair_dst[1]).reshape(8, 8, N)
    y1 = ring8(1, on_y, y, y1_src, y1_dst)
    pair[0].wait_recv()
    v = pair_src[0, c] + pair_dst[0]
    for xx in range(X):
        x0_src[xx] = quarter(v, xx)
    x0 = ring4(0, lambda t: x0_src.at[t], x0_dst)

    y0_src[...] = total(x0_src[x], x0, x0_dst).reshape(8, 8, 128)
    y0 = ring8(2, on_y, y, y0_src, y0_dst)
    v = total(y1_src[y], y1, y1_dst)
    for k in range(8):
        z1_src[k] = v[k:k + 1, :]
    z1 = ring8(3, on_z, z, z1_src, z1_dst)
    v = total(z2_src[z], z2, z2_dst)
    for xx in range(X):
        x2_src[xx] = quarter(v, xx)
    x2 = ring4(1, lambda t: x2_src.at[t], x2_dst)

    v = total(y0_src[y], y0, y0_dst)
    for k in range(8):
        z0_src[k] = v[k:k + 1, :]
    z0 = ring8(4, on_z, z, z0_src, z0_dst)
    v = total(x2_src[x], x2, x2_dst)
    for k in range(8):
        y2_src[k] = v[k:k + 1, :]
    y2 = ring8(5, on_y, y, y2_src, y2_dst)
    x1_src[...] = total(z1_src[z], z1, z1_dst)
    x1 = ring4(2, lambda t: x1_src, x1_dst)

    v = total(z0_src[z], z0, z0_dst)
    o_ref[0:1, :] = v[:, :COLS]
    v = total(y2_src[y], y2, y2_dst)
    o_ref[2:3, :] = v[:, :COLS]
    v = total(x1_src[...], x1, x1_dst)
    pick = quarter(v, 0)
    for xx in range(1, X):
        pick = jnp.where(x == xx, quarter(v, xx), pick)
    o_ref[1:2, :] = pick[:, :COLS]

    for i in range(SUB):
        pair[i].wait_send()
    for cp in sent:
        cp.wait_send()


def shards(factors, response, pattern):
    nocc_dev, aux_dev, nbasis = factors.shape
    rows = nocc_dev * aux_dev
    vm = pltpu.VMEM
    bf = factors.dtype
    scratch = [
        vm((rows, nbasis), bf), vm((rows, nbasis), bf), pltpu.SMEM(pattern.shape, jnp.int32),
        vm((pattern.shape[0], N, N // pattern.shape[0]), F32),
        vm((SUB, C, 64, N), F32), vm((SUB, 64, N), F32),
        vm((X, 64, 128), F32), vm((3, 64, 128), F32),
        vm((8, 8, 128), F32), vm((7, 8, 128), F32),
        vm((8, 1, 128), F32), vm((7, 1, 128), F32),
        vm((8, 8, N), F32), vm((7, 8, N), F32),
        vm((8, 1, N), F32), vm((7, 1, N), F32),
        vm((1, N), F32), vm((3, 1, N), F32),
        vm((8, 8, N), F32), vm((7, 8, N), F32),
        vm((X, 8, 128), F32), vm((3, 8, 128), F32),
        vm((8, 1, 128), F32), vm((7, 1, 128), F32),
        pltpu.SemaphoreType.DMA((5,)),
        pltpu.SemaphoreType.DMA((SUB,)), pltpu.SemaphoreType.DMA((SUB,)),
        pltpu.SemaphoreType.DMA((3, 3)), pltpu.SemaphoreType.DMA((3, 3)),
        pltpu.SemaphoreType.DMA((6, 7)), pltpu.SemaphoreType.DMA((6, 7)),
    ]
    return pl.pallas_call(
        kernel,
        out_shape=jax.ShapeDtypeStruct((SUB, COLS), F32),
        in_specs=[pl.BlockSpec(memory_space=pl.ANY)] * 3,
        out_specs=pl.BlockSpec(memory_space=pltpu.VMEM),
        scratch_shapes=scratch,
        compiler_params=pltpu.CompilerParams(collective_id=0, has_side_effects=True),
        name="exchange",
    )(factors.reshape(rows, nbasis), response.reshape(rows, nbasis), pattern)


def solution(mesh):
    in_specs = (P("occ", "aux", None), P("occ", "aux", None), P())
    out_specs = P("aux", "occ")
    return jax.shard_map(shards, mesh=mesh, in_specs=in_specs, out_specs=out_specs, check_vma=False)
```

time: 255 us -> 31.6 us (0.12)
  waiting for transfers between devices: 213 us -> 0 us
  Pallas kernels: 0 us -> 30.2 us
  between operations: 14.1 us -> 0.01 us
  starting transfers between devices: 8.84 us -> 0 us
  blocking collectives: 8.49 us -> 0 us
  local copies, waits for them, and re-layouts: 5.79 us -> 1.26 us
    unnamed x2 -> x0, waiting for transfers between devices: 199 us -> none
    pallas_call x0 -> x1, Pallas kernels: none -> 30.2 us  [shards(): pl.pallas_call(kernel, out_shape=jax.ShapeDtypeStruct((SUB, COLS), F32),...]
    all_to_all x1 -> x0, waiting for transfers between devices: 14.2 us -> none  [shards(): lax.all_to_all(own_rows, 'aux', split_axis=1, concat_axis=0, tiled=True)]
    all_to_all x1 -> x0, starting transfers between devices: 8.83 us -> none  [shards(): lax.all_to_all(own_rows, 'aux', split_axis=1, concat_axis=0, tiled=True)]
    psum x1 -> x0, blocking collectives: 8.49 us -> none  [shards(): summed = lax.psum(own_rows, 'occ')]
  transfers between devices with their start and end apart: 2 -> 0, of which waited for: 2 -> 0; matrix products, arithmetic and copies ran while one was open for 1% -> 0% of each run, Pallas kernels for 0% -> 0%
where the time goes in v1:
time: 31.6 us; the launch traced here: 31.5 us
  Pallas kernels  30.2 us (96%)
  local copies, waits for them, and re-layouts  1.26 us (4%)
    pallas_call x1, Pallas kernels, shards(): pl.pallas_call(kernel, out_shape=jax.ShapeDtypeStruct((SUB, COLS), F32),...  30.2 us
    unnamed x1, local copies, waits for them, and re-layouts  1.26 us

profile of v1, /device:TPU:1, one launch (start us, length us, event | category | flops | bytes accessed | tf_op | source)
XLA Modules:
  0.0 31.5 jit_solution(14179883167237183485)
XLA Ops:
  0.0 30.2 %exchange.1 = f32[3,96]{1,0:T(4,128)} custom-call(bf16[1024,384]{1,0:T(8,128)(2,1)} %bitcast.2, bf16[1024,384]{1,0:T(8,128)(2,1)} %bitcast.3, s32[3,3]{1,0:T(4,128)} %p_hbm.1), custom_call_target="tpu_custom_call" | custom-call | tf_op jit(solution)/shard_map/exchange/pallas_call | solution.py:218
  30.2 1.3 %copy.5 = f32[3,96]{1,0:T(4,128)} copy(f32[3,96]{1,0:T(4,128)} %exchange.1) | data formatting | bytes 2304

commit v2 on v1

--- a/solution.py
+++ b/solution.py
@@ -217,7 +217,7 @@
     ]
     return pl.pallas_call(
         kernel,
-        out_shape=jax.ShapeDtypeStruct((SUB, COLS), F32),
+        out_shape=pltpu.VMEM((SUB, COLS), F32),
         in_specs=[pl.BlockSpec(memory_space=pl.ANY)] * 3,
         out_specs=pl.BlockSpec(memory_space=pltpu.VMEM),
         scratch_shapes=scratch,

time: 31.6 us -> 30.3 us (0.959)
  local copies, waits for them, and re-layouts: 1.26 us -> 0.58 us
  Pallas kernels: 30.2 us -> 29.6 us
    unnamed x1, local copies, waits for them, and re-layouts: 1.26 us -> 0.58 us
    pallas_call x1, Pallas kernels: 30.2 us -> 29.6 us  [shards(): pl.pallas_call(kernel, out_shape=pltpu.VMEM((SUB, COLS), F32), in_specs=[...]
where the time goes in v2:
time: 30.3 us; the launch traced here: 30.2 us
  Pallas kernels  29.6 us (98%)
  local copies, waits for them, and re-layouts  0.58 us (2%)
    pallas_call x1, Pallas kernels, shards(): pl.pallas_call(kernel, out_shape=pltpu.VMEM((SUB, COLS), F32), in_specs=[...  29.6 us

profile of v2, /device:TPU:1, one launch (start us, length us, event | category | flops | bytes accessed | tf_op | source)
XLA Modules:
  0.0 30.2 jit_solution(1073787492813415727)
XLA Ops:
  0.0 29.6 %exchange.1 = f32[3,96]{1,0:T(4,128)S(1)} custom-call(bf16[1024,384]{1,0:T(8,128)(2,1)} %bitcast.2, bf16[1024,384]{1,0:T(8,128)(2,1)} %bitcast.3, s32[3,3]{1,0:T(4,128)} %p_hbm.1), custom_call_target="tpu_custom_call" | custom-call | tf_op jit(solution)/shard_map/exchange/pallas_call | solution.py:218
  29.6 0.6 %copy.5 = f32[3,96]{1,0:T(4,128)} copy(f32[3,96]{1,0:T(4,128)S(1)} %exchange.1) | data formatting | bytes 2304

commit v3 on v2

--- a/solution.py
+++ b/solution.py
@@ -14,14 +14,18 @@
 FAR4 = (2, 1, 3)
 
 
+def plane(n, m):
+    steps = [(j, k) for j in range(n) for k in range(m) if j or k]
+    return sorted(steps, key=lambda s: (-min(s[0], n - s[0]) - min(s[1], m - s[1]), s))
+
+
 def kernel(
     a_hbm, b_hbm, p_hbm, o_ref,
     a_v, b_v, p_s, t_v,
     pair_src, pair_dst,
-    x0_src, x0_dst, y0_src, y0_dst, z0_src, z0_dst,
-    y1_src, y1_dst, z1_src, z1_dst, x1_src, x1_dst,
-    z2_src, z2_dst, x2_src, x2_dst, y2_src, y2_dst,
-    load_sem, pair_send, pair_recv, send4, recv4, send8, recv8,
+    x0_src, x0_dst, y1_src, y1_dst, z2_src, z2_dst,
+    p0_src, p0_dst, p1_src, p1_dst, p2_src, p2_dst,
+    load_sem, pair_send, pair_recv, send4, recv4, send8, recv8, plane_send, plane_recv, hello,
 ):
     aux = lax.axis_index("aux")
     x = lax.axis_index("occ")
@@ -32,14 +36,18 @@
     def at(x_, y_, z_, c_):
         return ((y_ * Z + z_) * C + c_, x_)
 
+    xs = [x if k == 0 else lax.rem(x + k, X) for k in range(X)]
+    ys = [y if k == 0 else lax.rem(y + k, Y) for k in range(Y)]
+    zs = [z if k == 0 else lax.rem(z + k, Z) for k in range(Z)]
+
     def on_x(k):
-        return at(lax.rem(x + k, X), y, z, c)
+        return at(xs[k], y, z, c)
 
     def on_y(k):
-        return at(x, lax.rem(y + k, Y), z, c)
+        return at(x, ys[k], z, c)
 
     def on_z(k):
-        return at(x, y, lax.rem(z + k, Z), c)
+        return at(x, y, zs[k], c)
 
     partner = at(x, y, z, 1 - c)
 
@@ -106,13 +114,16 @@
         )
         pair[i].start()
 
+    for k in FAR8:
+        pl.semaphore_signal(hello, inc=1, device_id=on_z(k), device_id_type=pl.DeviceIdType.MESH)
+
     sent = []
 
-    def ring8(slot, to, me, src, dst):
+    def ring8(slot, to, steps, src, dst):
         out = {}
         for k in FAR8:
             cp = remote(
-                src.at[lax.rem(me + k, 8)], dst.at[k - 1],
+                src.at[steps[k]], dst.at[k - 1],
                 send8.at[slot, k - 1], recv8.at[slot, k - 1], to(k),
             )
             cp.start()
@@ -120,17 +131,17 @@
         sent.extend(out.values())
         return out
 
-    def ring4(slot, src, dst):
-        out = {}
-        for k in FAR4:
-            cp = remote(
-                src(lax.rem(x + k, X)), dst.at[k - 1],
-                send4.at[slot, k - 1], recv4.at[slot, k - 1], on_x(k),
-            )
-            cp.start()
-            out[k] = cp
-        sent.extend(out.values())
-        return out
+    def over_plane(slot, order, width, src, dst, pick, to):
+        for j, k in order:
+            remote(
+                src.at[pick(j, k)], dst.at[j * width + k], plane_send.at[slot], plane_recv.at[slot], to(j, k)
+            ).start()
+        n = len(order)
+        everything = remote(
+            src.at[pl.ds(1, n)], dst.at[pl.ds(1, n)], plane_send.at[slot], plane_recv.at[slot], partner
+        )
+        sent.append(everything)
+        return everything
 
     def total(own, copies, dst):
         acc = own
@@ -144,47 +155,55 @@
 
     pair[2].wait_recv()
     z2_src[...] = (pair_src[2, c] + pair_dst[2]).reshape(8, 8, N)
-    z2 = ring8(0, on_z, z, z2_src, z2_dst)
+    z2 = ring8(0, on_z, zs, z2_src, z2_dst)
     pair[1].wait_recv()
     y1_src[...] = (pair_src[1, c] + pair_dst[1]).reshape(8, 8, N)
-    y1 = ring8(1, on_y, y, y1_src, y1_dst)
+    y1 = ring8(1, on_y, ys, y1_src, y1_dst)
     pair[0].wait_recv()
     v = pair_src[0, c] + pair_dst[0]
     for xx in range(X):
         x0_src[xx] = quarter(v, xx)
-    x0 = ring4(0, lambda t: x0_src.at[t], x0_dst)
-
-    y0_src[...] = total(x0_src[x], x0, x0_dst).reshape(8, 8, 128)
-    y0 = ring8(2, on_y, y, y0_src, y0_dst)
-    v = total(y1_src[y], y1, y1_dst)
-    for k in range(8):
-        z1_src[k] = v[k:k + 1, :]
-    z1 = ring8(3, on_z, z, z1_src, z1_dst)
+    x0 = {}
+    for k in FAR4:
+        x0[k] = remote(x0_src.at[xs[k]], x0_dst.at[k - 1], send4.at[k - 1], recv4.at[k - 1], on_x(k))
+        x0[k].start()
+    sent.extend(x0.values())
+
+    v = total(x0_src[x], x0, x0_dst)
+    for r in range(Y * Z):
+        p0_src[r] = v[r:r + 1, :]
+    pl.semaphore_wait(hello, len(FAR8))
+    p0 = over_plane(
+        0, plane(Y, Z), Z, p0_src, p0_dst,
+        lambda j, k: ys[j] * Z + zs[k], lambda j, k: at(x, ys[j], zs[k], c),
+    )
+    p0_dst[0] = p0_src[y * Z + z]
+
     v = total(z2_src[z], z2, z2_dst)
     for xx in range(X):
-        x2_src[xx] = quarter(v, xx)
-    x2 = ring4(1, lambda t: x2_src.at[t], x2_dst)
-
-    v = total(y0_src[y], y0, y0_dst)
-    for k in range(8):
-        z0_src[k] = v[k:k + 1, :]
-    z0 = ring8(4, on_z, z, z0_src, z0_dst)
-    v = total(x2_src[x], x2, x2_dst)
-    for k in range(8):
-        y2_src[k] = v[k:k + 1, :]
-    y2 = ring8(5, on_y, y, y2_src, y2_dst)
-    x1_src[...] = total(z1_src[z], z1, z1_dst)
-    x1 = ring4(2, lambda t: x1_src, x1_dst)
-
-    v = total(z0_src[z], z0, z0_dst)
-    o_ref[0:1, :] = v[:, :COLS]
-    v = total(y2_src[y], y2, y2_dst)
-    o_ref[2:3, :] = v[:, :COLS]
-    v = total(x1_src[...], x1, x1_dst)
-    pick = quarter(v, 0)
-    for xx in range(1, X):
-        pick = jnp.where(x == xx, quarter(v, xx), pick)
-    o_ref[1:2, :] = pick[:, :COLS]
+        q = quarter(v, xx)
+        for r in range(Y):
+            p2_src[xx * Y + r] = q[r:r + 1, :]
+    p2 = over_plane(
+        2, plane(X, Y), Y, p2_src, p2_dst,
+        lambda j, k: xs[j] * Y + ys[k], lambda j, k: at(xs[j], ys[k], z, c),
+    )
+    p2_dst[0] = p2_src[x * Y + y]
+
+    v = total(y1_src[y], y1, y1_dst)
+    for xx in range(X):
+        q = quarter(v, xx)
+        for r in range(Z):
+            p1_src[xx * Z + r] = q[r:r + 1, :]
+    p1 = over_plane(
+        1, plane(X, Z), Z, p1_src, p1_dst,
+        lambda j, k: xs[j] * Z + zs[k], lambda j, k: at(xs[j], y, zs[k], c),
+    )
+    p1_dst[0] = p1_src[x * Z + z]
+
+    for i, (cp, dst) in ((2, (p2, p2_dst)), (1, (p1, p1_dst)), (0, (p0, p0_dst))):
+        cp.wait_recv()
+        o_ref[i:i + 1, :] = jnp.sum(dst[...], axis=0)[:, :COLS]
 
     for i in range(SUB):
         pair[i].wait_send()
@@ -202,18 +221,17 @@
         vm((pattern.shape[0], N, N // pattern.shape[0]), F32),
         vm((SUB, C, 64, N), F32), vm((SUB, 64, N), F32),
         vm((X, 64, 128), F32), vm((3, 64, 128), F32),
-        vm((8, 8, 128), F32), vm((7, 8, 128), F32),
-        vm((8, 1, 128), F32), vm((7, 1, 128), F32),
         vm((8, 8, N), F32), vm((7, 8, N), F32),
-        vm((8, 1, N), F32), vm((7, 1, N), F32),
-        vm((1, N), F32), vm((3, 1, N), F32),
         vm((8, 8, N), F32), vm((7, 8, N), F32),
-        vm((X, 8, 128), F32), vm((3, 8, 128), F32),
-        vm((8, 1, 128), F32), vm((7, 1, 128), F32),
+        vm((Y * Z, 1, 128), F32), vm((Y * Z, 1, 128), F32),
+        vm((X * Z, 1, 128), F32), vm((X * Z, 1, 128), F32),
+        vm((X * Y, 1, 128), F32), vm((X * Y, 1, 128), F32),
         pltpu.SemaphoreType.DMA((5,)),
         pltpu.SemaphoreType.DMA((SUB,)), pltpu.SemaphoreType.DMA((SUB,)),
-        pltpu.SemaphoreType.DMA((3, 3)), pltpu.SemaphoreType.DMA((3, 3)),
-        pltpu.SemaphoreType.DMA((6, 7)), pltpu.SemaphoreType.DMA((6, 7)),
+        pltpu.SemaphoreType.DMA((3,)), pltpu.SemaphoreType.DMA((3,)),
+        pltpu.SemaphoreType.DMA((2, 7)), pltpu.SemaphoreType.DMA((2, 7)),
+        pltpu.SemaphoreType.DMA((3,)), pltpu.SemaphoreType.DMA((3,)),
+        pltpu.SemaphoreType.REGULAR,
     ]
     return pl.pallas_call(
         kernel,

time: 30.3 us -> 28.3 us (0.934)
  Pallas kernels: 29.6 us -> 27.5 us
    pallas_call x1, Pallas kernels: 29.6 us -> 27.5 us  [shards(): pl.pallas_call(kernel, out_shape=pltpu.VMEM((SUB, COLS), F32), in_specs=[...]
where the time goes in v3:
time: 28.3 us; the launch traced here: 28.1 us
  Pallas kernels  27.5 us (97%)
  local copies, waits for them, and re-layouts  0.58 us (2%)
    pallas_call x1, Pallas kernels, shards(): pl.pallas_call(kernel, out_shape=pltpu.VMEM((SUB, COLS), F32), in_specs=[...  27.5 us
    unnamed x1, local copies, waits for them, and re-layouts  0.58 us

profile of v3, /device:TPU:1, one launch (start us, length us, event | category | flops | bytes accessed | tf_op | source)
XLA Modules:
  0.0 28.1 jit_solution(15662842137850405176)
XLA Ops:
  0.0 27.5 %exchange.1 = f32[3,96]{1,0:T(4,128)S(1)} custom-call(bf16[1024,384]{1,0:T(8,128)(2,1)} %bitcast.2, bf16[1024,384]{1,0:T(8,128)(2,1)} %bitcast.3, s32[3,3]{1,0:T(4,128)} %p_hbm.1), custom_call_target="tpu_custom_call" | custom-call | tf_op jit(solution)/shard_map/exchange/pallas_call | solution.py:236
  27.5 0.6 %copy.5 = f32[3,96]{1,0:T(4,128)} copy(f32[3,96]{1,0:T(4,128)S(1)} %exchange.1) | data formatting | bytes 2304

commit v4 on v3

--- a/solution.py
+++ b/solution.py
@@ -9,9 +9,12 @@
 SUB = 3
 N = 384
 COLS = N // X
+PARTS = 4
 F32 = jnp.float32
 FAR8 = (4, 3, 5, 2, 6, 1, 7)
 FAR4 = (2, 1, 3)
+NEAR8 = (2, 6, 1, 7)
+VOUCH8 = (2, 6)
 
 
 def plane(n, m):
@@ -25,7 +28,7 @@
     pair_src, pair_dst,
     x0_src, x0_dst, y1_src, y1_dst, z2_src, z2_dst,
     p0_src, p0_dst, p1_src, p1_dst, p2_src, p2_dst,
-    load_sem, pair_send, pair_recv, send4, recv4, send8, recv8, plane_send, plane_recv, hello,
+    load_sem, pair_send, pair_recv, send4, recv4, send8, recv8, plane_send, plane_recv, vouch, hello,
 ):
     aux = lax.axis_index("aux")
     x = lax.axis_index("occ")
@@ -52,32 +55,38 @@
     partner = at(x, y, z, 1 - c)
 
     rows = a_v.shape[0]
-    half = rows // 2
+    part = rows // PARTS
     loads = []
-    for h in range(2):
-        part = pl.ds(h * half, half)
+    for h in range(PARTS):
+        here = pl.ds(h * part, part)
         for n, (src, dst) in enumerate(((a_hbm, a_v), (b_hbm, b_v))):
-            loads.append(pltpu.make_async_copy(src.at[part], dst.at[part], load_sem.at[2 * h + n]))
-    p_load = pltpu.make_async_copy(p_hbm, p_s, load_sem.at[4])
+            loads.append(pltpu.make_async_copy(src.at[here], dst.at[here], load_sem.at[2 * h + n]))
+    p_load = pltpu.make_async_copy(p_hbm, p_s, load_sem.at[2 * PARTS])
     for ld in loads:
         ld.start()
     p_load.start()
 
     barrier = pltpu.get_barrier_semaphore()
     greeted = [partner]
-    greeted += [on_y(k) for k in FAR8] + [on_z(k) for k in FAR8] + [on_x(k) for k in FAR4]
+    greeted += [on(k) for k in NEAR8 for on in (on_y, on_z)] + [on_x(k) for k in FAR4]
     for who in greeted:
         pl.semaphore_signal(barrier, inc=1, device_id=who, device_id_type=pl.DeviceIdType.MESH)
 
     def dot_t(l, r):
         return lax.dot_general(l, r, (((0,), (0,)), ((), ())), preferred_element_type=F32)
 
-    loads[0].wait()
-    loads[1].wait()
-    s = dot_t(a_v[:half], b_v[:half])
-    loads[2].wait()
-    loads[3].wait()
-    s = s + dot_t(a_v[half:], b_v[half:])
+    s = 0.0
+    for h in range(PARTS - 1):
+        loads[2 * h].wait()
+        loads[2 * h + 1].wait()
+        s = s + dot_t(a_v[h * part:(h + 1) * part], b_v[h * part:(h + 1) * part])
+    pl.semaphore_wait(barrier, len(greeted))
+    vouchers = [on(k) for k in VOUCH8 for on in (on_y, on_z)]
+    for who in vouchers:
+        pl.semaphore_signal(vouch, inc=1, device_id=who, device_id_type=pl.DeviceIdType.MESH)
+    loads[-2].wait()
+    loads[-1].wait()
+    s = s + dot_t(a_v[rows - part:], b_v[rows - part:])
     p_load.wait()
     nb = p_s.shape[0]
     blk = N // nb
@@ -106,16 +115,12 @@
         )
 
     pair = {}
-    pl.semaphore_wait(barrier, len(greeted))
     for i in (2, 1, 0):
         pack(i)
         pair[i] = remote(
             pair_src.at[i, 1 - c], pair_dst.at[i], pair_send.at[i], pair_recv.at[i], partner
         )
         pair[i].start()
-
-    for k in FAR8:
-        pl.semaphore_signal(hello, inc=1, device_id=on_z(k), device_id_type=pl.DeviceIdType.MESH)
 
     sent = []
 
@@ -153,6 +158,7 @@
     def quarter(v, xx):
         return pltpu.roll(v, (N - COLS * xx) % N, 1)[:, :128] if xx else v[:, :128]
 
+    pl.semaphore_wait(vouch, len(vouchers))
     pair[2].wait_recv()
     z2_src[...] = (pair_src[2, c] + pair_dst[2]).reshape(8, 8, N)
     z2 = ring8(0, on_z, zs, z2_src, z2_dst)
@@ -169,6 +175,9 @@
         x0[k].start()
     sent.extend(x0.values())
 
+    for k in FAR8:
+        pl.semaphore_signal(hello, inc=1, device_id=on_z(k), device_id_type=pl.DeviceIdType.MESH)
+
     v = total(x0_src[x], x0, x0_dst)
     for r in range(Y * Z):
         p0_src[r] = v[r:r + 1, :]
@@ -226,12 +235,12 @@
         vm((Y * Z, 1, 128), F32), vm((Y * Z, 1, 128), F32),
         vm((X * Z, 1, 128), F32), vm((X * Z, 1, 128), F32),
         vm((X * Y, 1, 128), F32), vm((X * Y, 1, 128), F32),
-        pltpu.SemaphoreType.DMA((5,)),
+        pltpu.SemaphoreType.DMA((2 * PARTS + 1,)),
         pltpu.SemaphoreType.DMA((SUB,)), pltpu.SemaphoreType.DMA((SUB,)),
         pltpu.SemaphoreType.DMA((3,)), pltpu.SemaphoreType.DMA((3,)),
         pltpu.SemaphoreType.DMA((2, 7)), pltpu.SemaphoreType.DMA((2, 7)),
         pltpu.SemaphoreType.DMA((3,)), pltpu.SemaphoreType.DMA((3,)),
-        pltpu.SemaphoreType.REGULAR,
+        pltpu.SemaphoreType.REGULAR, pltpu.SemaphoreType.REGULAR,
     ]
     return pl.pallas_call(
         kernel,

time: 28.3 us -> 27.3 us (0.965)
  Pallas kernels: 27.5 us -> 26.6 us
    pallas_call x1, Pallas kernels: 27.5 us -> 26.6 us  [shards(): pl.pallas_call(kernel, out_shape=pltpu.VMEM((SUB, COLS), F32), in_specs=[...]
where the time goes in v4:
time: 27.3 us; the launch traced here: 27.2 us
  Pallas kernels  26.6 us (97%)
  local copies, waits for them, and re-layouts  0.58 us (2%)
    pallas_call x1, Pallas kernels, shards(): pl.pallas_call(kernel, out_shape=pltpu.VMEM((SUB, COLS), F32), in_specs=[...  26.6 us
    unnamed x1, local copies, waits for them, and re-layouts  0.58 us

profile of v4, /device:TPU:1, one launch (start us, length us, event | category | flops | bytes accessed | tf_op | source)
XLA Modules:
  0.0 27.2 jit_solution(11723288944945710322)
XLA Ops:
  0.0 26.6 %exchange.1 = f32[3,96]{1,0:T(4,128)S(1)} custom-call(bf16[1024,384]{1,0:T(8,128)(2,1)} %bitcast.2, bf16[1024,384]{1,0:T(8,128)(2,1)} %bitcast.3, s32[3,3]{1,0:T(4,128)} %p_hbm.1), custom_call_target="tpu_custom_call" | custom-call | tf_op jit(solution)/shard_map/exchange/pallas_call | solution.py:245
  26.6 0.6 %copy.5 = f32[3,96]{1,0:T(4,128)} copy(f32[3,96]{1,0:T(4,128)S(1)} %exchange.1) | data formatting | bytes 2304

commit v5 on v4

--- a/solution.py
+++ b/solution.py
@@ -15,6 +15,7 @@
 FAR4 = (2, 1, 3)
 NEAR8 = (2, 6, 1, 7)
 VOUCH8 = (2, 6)
+REST8 = (4, 3, 5)
 
 
 def plane(n, m):
@@ -68,7 +69,7 @@
 
     barrier = pltpu.get_barrier_semaphore()
     greeted = [partner]
-    greeted += [on(k) for k in NEAR8 for on in (on_y, on_z)] + [on_x(k) for k in FAR4]
+    greeted += [on(k) for k in NEAR8 for on in (on_z, on_y)] + [on_x(k) for k in FAR4]
     for who in greeted:
         pl.semaphore_signal(barrier, inc=1, device_id=who, device_id_type=pl.DeviceIdType.MESH)
 
@@ -76,17 +77,16 @@
         return lax.dot_general(l, r, (((0,), (0,)), ((), ())), preferred_element_type=F32)
 
     s = 0.0
+    st = 0.0
     for h in range(PARTS - 1):
         loads[2 * h].wait()
         loads[2 * h + 1].wait()
         s = s + dot_t(a_v[h * part:(h + 1) * part], b_v[h * part:(h + 1) * part])
-    pl.semaphore_wait(barrier, len(greeted))
-    vouchers = [on(k) for k in VOUCH8 for on in (on_y, on_z)]
-    for who in vouchers:
-        pl.semaphore_signal(vouch, inc=1, device_id=who, device_id_type=pl.DeviceIdType.MESH)
+        st = st + dot_t(b_v[h * part:(h + 1) * part], a_v[h * part:(h + 1) * part])
     loads[-2].wait()
     loads[-1].wait()
     s = s + dot_t(a_v[rows - part:], b_v[rows - part:])
+    st = st + dot_t(b_v[rows - part:], a_v[rows - part:])
     p_load.wait()
     nb = p_s.shape[0]
     blk = N // nb
@@ -95,7 +95,7 @@
             f_ij = 0.5 * p_s[i, j].astype(F32)
             f_ji = 0.5 * p_s[j, i].astype(F32)
             r_i, r_j = slice(i * blk, (i + 1) * blk), slice(j * blk, (j + 1) * blk)
-            t_v[j, r_i, :] = f_ij * s[r_i, r_j] + f_ji * s[r_j, r_i].T
+            t_v[j, r_i, :] = f_ij * s[r_i, r_j] + f_ji * st[r_i, r_j]
 
     def pack(i):
         for cc in range(C):
@@ -114,6 +114,10 @@
             device_id=who, device_id_type=pl.DeviceIdType.MESH,
         )
 
+    pl.semaphore_wait(barrier, len(greeted))
+    vouchers = [on(k) for k in VOUCH8 for on in (on_z, on_y)]
+    for who in vouchers:
+        pl.semaphore_signal(vouch, inc=1, device_id=who, device_id_type=pl.DeviceIdType.MESH)
     pair = {}
     for i in (2, 1, 0):
         pack(i)
@@ -124,9 +128,9 @@
 
     sent = []
 
-    def ring8(slot, to, steps, src, dst):
+    def ring8(slot, to, steps, src, dst, some):
         out = {}
-        for k in FAR8:
+        for k in some:
             cp = remote(
                 src.at[steps[k]], dst.at[k - 1],
                 send8.at[slot, k - 1], recv8.at[slot, k - 1], to(k),
@@ -158,13 +162,14 @@
     def quarter(v, xx):
         return pltpu.roll(v, (N - COLS * xx) % N, 1)[:, :128] if xx else v[:, :128]
 
-    pl.semaphore_wait(vouch, len(vouchers))
     pair[2].wait_recv()
     z2_src[...] = (pair_src[2, c] + pair_dst[2]).reshape(8, 8, N)
-    z2 = ring8(0, on_z, zs, z2_src, z2_dst)
+    z2 = ring8(0, on_z, zs, z2_src, z2_dst, NEAR8)
+    pl.semaphore_wait(vouch, len(vouchers))
+    z2 |= ring8(0, on_z, zs, z2_src, z2_dst, REST8)
     pair[1].wait_recv()
     y1_src[...] = (pair_src[1, c] + pair_dst[1]).reshape(8, 8, N)
-    y1 = ring8(1, on_y, ys, y1_src, y1_dst)
+    y1 = ring8(1, on_y, ys, y1_src, y1_dst, FAR8)
     pair[0].wait_recv()
     v = pair_src[0, c] + pair_dst[0]
     for xx in range(X):
@@ -210,14 +215,14 @@
     )
     p1_dst[0] = p1_src[x * Z + z]
 
-    for i, (cp, dst) in ((2, (p2, p2_dst)), (1, (p1, p1_dst)), (0, (p0, p0_dst))):
-        cp.wait_recv()
-        o_ref[i:i + 1, :] = jnp.sum(dst[...], axis=0)[:, :COLS]
-
     for i in range(SUB):
         pair[i].wait_send()
     for cp in sent:
         cp.wait_send()
+
+    for i, (cp, dst) in ((2, (p2, p2_dst)), (1, (p1, p1_dst)), (0, (p0, p0_dst))):
+        cp.wait_recv()
+        o_ref[i:i + 1, :] = jnp.sum(dst[...], axis=0)[:, :COLS]
 
 
 def shards(factors, response, pattern):

time: 27.3 us -> 27.2 us (level)
  no operation moved by 1% of the time
where the time goes in v5:
time: 27.2 us; the launch traced here: 27 us
  Pallas kernels  26.4 us (97%)
  local copies, waits for them, and re-layouts  0.58 us (2%)
    pallas_call x1, Pallas kernels, shards(): pl.pallas_call(kernel, out_shape=pltpu.VMEM((SUB, COLS), F32), in_specs=[...  26.4 us
    unnamed x1, local copies, waits for them, and re-layouts  0.58 us

profile of v5, /device:TPU:1, one launch (start us, length us, event | category | flops | bytes accessed | tf_op | source)
XLA Modules:
  0.0 27.0 jit_solution(18401384055626819474)
XLA Ops:
  0.0 26.4 %exchange.1 = f32[3,96]{1,0:T(4,128)S(1)} custom-call(bf16[1024,384]{1,0:T(8,128)(2,1)} %bitcast.2, bf16[1024,384]{1,0:T(8,128)(2,1)} %bitcast.3, s32[3,3]{1,0:T(4,128)} %p_hbm.1), custom_call_target="tpu_custom_call" | custom-call | tf_op jit(solution)/shard_map/exchange/pallas_call | solution.py:250
  26.4 0.6 %copy.5 = f32[3,96]{1,0:T(4,128)} copy(f32[3,96]{1,0:T(4,128)S(1)} %exchange.1) | data formatting | bytes 2304

commit v6 on v5

--- a/solution.py
+++ b/solution.py
@@ -170,6 +170,9 @@
     pair[1].wait_recv()
     y1_src[...] = (pair_src[1, c] + pair_dst[1]).reshape(8, 8, N)
     y1 = ring8(1, on_y, ys, y1_src, y1_dst, FAR8)
+    for k in FAR8:
+        pl.semaphore_signal(hello, inc=1, device_id=on_z(k), device_id_type=pl.DeviceIdType.MESH)
+
     pair[0].wait_recv()
     v = pair_src[0, c] + pair_dst[0]
     for xx in range(X):
@@ -179,9 +182,6 @@
         x0[k] = remote(x0_src.at[xs[k]], x0_dst.at[k - 1], send4.at[k - 1], recv4.at[k - 1], on_x(k))
         x0[k].start()
     sent.extend(x0.values())
-
-    for k in FAR8:
-        pl.semaphore_signal(hello, inc=1, device_id=on_z(k), device_id_type=pl.DeviceIdType.MESH)
 
     v = total(x0_src[x], x0, x0_dst)
     for r in range(Y * Z):

time: 27.2 us -> 27.2 us (level)
  no operation moved by 1% of the time
where the time goes in v6:
time: 27.2 us; the launch traced here: 27 us
  Pallas kernels  26.4 us (97%)
  local copies, waits for them, and re-layouts  0.58 us (2%)
    pallas_call x1, Pallas kernels, shards(): pl.pallas_call(kernel, out_shape=pltpu.VMEM((SUB, COLS), F32), in_specs=[...  26.4 us
    unnamed x1, local copies, waits for them, and re-layouts  0.58 us

profile of v6, /device:TPU:1, one launch (start us, length us, event | category | flops | bytes accessed | tf_op | source)
XLA Modules:
  0.0 27.0 jit_solution(3872268459772453936)
XLA Ops:
  0.0 26.4 %exchange.1 = f32[3,96]{1,0:T(4,128)S(1)} custom-call(bf16[1024,384]{1,0:T(8,128)(2,1)} %bitcast.2, bf16[1024,384]{1,0:T(8,128)(2,1)} %bitcast.3, s32[3,3]{1,0:T(4,128)} %p_hbm.1), custom_call_target="tpu_custom_call" | custom-call | tf_op jit(solution)/shard_map/exchange/pallas_call | solution.py:250
  26.4 0.6 %copy.5 = f32[3,96]{1,0:T(4,128)} copy(f32[3,96]{1,0:T(4,128)S(1)} %exchange.1) | data formatting | bytes 2304
